TPU v7x, 256 devices: a whole 4x4x8 slice. The times are simulated.
256 devices in a mesh: pix: 32 (over z, y), shell: 8 (over x, core).
Axes of the slice: x: 4, y: 4, z: 8, core: 2. Of those that a mesh axis runs over, the one named last changes fastest.
Arguments:
- field: float32 [128, 1048576], P('shell', 'pix'), may hold values from -3 to 3
- momentum: float32 [128, 1048576], P('shell', 'pix'), may hold values from -6 to 6
- kernels: float32 [4, 20, 128], P(None, None, 'shell'), may hold values from 0.002 to 0.02
- depth_class: int32 [1048576], P('pix'), may hold values from 0 to 3
- counts: int32 [20, 1048576], P(None, 'pix'), may hold values from 0 to 12
- mask: float32 [1048576], P('pix'), may hold values from 0.1 to 1.5, as said below
- mean_counts: float32 [20], replicated, may hold values from 1 to 8
- shell_scale: float32 [128], P('shell'), may hold values from 0.5 to 2
Outputs:
- gradient: float32 [128, 1048576], P('shell', 'pix')
- loglik: float32 [], replicated
Inputs may be any that keep to these rules, and one draw needn't show every extreme that they name: `mask`: mask weights are positive.
All inputs are finite; a program needn't handle non-finite values.
Results may differ from a plain program's by a relative error of at most 0.00005.
Values sent between devices are 32-bit elements; how exact they have to be, the bound alone decides.
No kernel may reach another device: no remote copies, remote signals or barrier semaphores. Data moves between devices by JAX's collectives and lax.ppermute only.
A program may use at most 128 MiB of HBM per device.

v0:
```python
import jax
import jax.numpy as jnp
from jax import lax
from jax.sharding import PartitionSpec as P

CYCLE = 2048
LEAP = 0.1
ANGULAR = 0.5
RADIAL = 0.5


def padded_2(cells, sides, width):
    for axis, dim in sides:
        count = lax.axis_size(axis)
        ends = count - 1
        head = lax.slice_in_dim(cells, 0, width, axis=dim)
        tail = lax.slice_in_dim(cells, cells.shape[dim] - width, cells.shape[dim], axis=dim)
        cells = jnp.concatenate(
            [
                lax.ppermute(tail, axis, [(i, (i + 1) % count) for i in range(ends)]),
                cells,
                lax.ppermute(head, axis, [((i + 1) % count, i) for i in range(ends)]),
            ],
            axis=dim,
        )
    return cells


def shards(field, momentum, kernels, depth_class, counts, mask, mean_counts, shell_scale):
    shells_here, pixels = field.shape
    classes, bins, _ = kernels.shape
    total_pix = pixels * lax.axis_size("pix")
    position = field + LEAP * momentum
    density = jnp.exp(position)
    flat = kernels.reshape(classes * bins, shells_here)
    onehot = (depth_class[None, :] == jnp.arange(classes, dtype=jnp.int32)[:, None]).astype(
        jnp.float32
    )
    every = jnp.dot(
        flat, density, precision=lax.Precision.HIGHEST, preferred_element_type=jnp.float32
    )
    partial_proj = jnp.sum(every.reshape(classes, bins, pixels) * onehot[:, None, :], axis=0)
    counted = counts.astype(jnp.float32)
    proj = lax.psum(partial_proj, "shell")
    weighted, total = lax.psum(
        (jnp.sum(mask[None, :] * proj, axis=1), jnp.sum(counted, axis=1)), "pix"
    )
    norm = weighted / total_pix
    rate = mean_counts[:, None] * mask[None, :] * proj / norm[:, None]
    local_sum = jnp.sum(counted * jnp.log(rate) - rate)
    loglik = lax.psum(local_sum, "pix") / (bins * total_pix)
    ratio = counted / proj - (total / (total_pix * norm))[:, None] * mask[None, :]
    padded = padded_2(position, (("pix", 1),), CYCLE)
    angular = (
        4.0 * position
        - padded[:, CYCLE - 1 : CYCLE - 1 + pixels]
        - padded[:, CYCLE + 1 : CYCLE + 1 + pixels]
    )
    angular = angular - padded[:, 0:pixels] - padded[:, 2 * CYCLE : 2 * CYCLE + pixels]
    stacked = padded_2(position, (("shell", 0),), 1)
    radial = 2.0 * position - stacked[:-2] - stacked[2:]
    spread = (onehot[:, None, :] * ratio[None, :, :]).reshape(classes * bins, pixels)
    back = lax.dot_general(
        flat,
        spread,
        (((0,), (0,)), ((), ())),
        precision=lax.Precision.HIGHEST,
        preferred_element_type=jnp.float32,
    )
    like = density * back
    gradient = (
        like
        - position / (shell_scale[:, None] * shell_scale[:, None])
        - ANGULAR * angular
        - RADIAL * radial
    )
    return (gradient, loglik)


def solution(mesh):
    placed = (
        P("shell", "pix"),
        P("shell", "pix"),
        P(None, None, "shell"),
        P("pix"),
        P(None, "pix"),
        P("pix"),
        P(),
        P("shell"),
    )
    return jax.shard_map(
        shards, mesh=mesh, in_specs=placed, out_specs=(P("shell", "pix"), P()), check_vma=False
    )
```

profile of v0, /device:TPU:8, one launch (start us, length us, event | category | flops | bytes accessed | tf_op | source)
XLA Modules:
  0.0 298.6 jit_solution(3591351216382486892)
XLA Ops:
  7.2 0.0 all-reduce.3.cloned.1.call-start
  7.2 0.8 copy.10
  8.0 0.1 reshape.36
  8.1 2.5 multiply_add_fusion
  10.5 0.0 copy-start.1
  10.5 10.9 %convolution_bitcast_fusion = f32[80,32768]{1,0:T(8,128)} fusion(f32[80,16]{0,1:T(8,128)S(1)} %reshape.36, f32[16,32768]{1,0:T(8,128)S(1)} %multiply_add_fusion), kind=kOutput, calls=%fused_computation | convolution fusion | flops 503316480 | bytes 12588032 | tf_op jit(solution)/shard_map/dot_general | solution.py:39
  21.4 0.0 copy-start.4
  21.4 11.4 %reshape.37 = f32[4,20,32768]{2,1,0:T(8,128)} reshape(f32[80,32768]{1,0:T(8,128)} %convolution_bitcast_fusion) | data formatting | bytes 20971520 | tf_op jit(solution)/shard_map/reshape | solution.py:42
  32.8 0.0 copy-done.4
  32.8 0.1 fusion.20
  32.9 0.0 copy-start.2
  32.9 0.8 copy-done.2
  33.7 8.0 %multiply_reduce_fusion = f32[20,32768]{1,0:T(8,128)} fusion(f32[4,20,32768]{2,1,0:T(8,128)} %reshape.37, f32[4,32768]{1,0:T(4,128)S(1)} %fusion.20), kind=kLoop, calls=%fused_computation.5 | loop fusion | flops 4587520 | bytes 13631488 | tf_op jit(solution)/shard_map/reduce_sum | solution.py:42
  41.7 0.0 copy-start.3
  41.7 0.0 all-reduce.3.cloned.1.call-update
  41.8 0.0 copy-start.6
  41.8 0.0 copy-start.5
  41.8 3.6 %collective-permute-start = (f32[16,2048]{1,0:T(8,128)S(1)}, f32[16,2048]{1,0:T(8,128)}, u32[]{:S(2)}, u32[]{:S(2)}) collective-permute-start(f32[16,2048]{1,0:T(8,128)S(1)} %get-tuple-element.8), channel_id=1, source_target_pairs={{0,8},{8,16},{16,24},{24,32},{32,40},{40,48},{48,56},{56,64},{64,7... | collective-permute-start | bytes 393224 | tf_op jit(solution)/shard_map/ppermute | solution.py:20
  45.4 3.0 %collective-permute-start.1 = (f32[16,2048]{1,0:T(8,128)S(1)}, f32[16,2048]{1,0:T(8,128)}, u32[]{:S(2)}, u32[]{:S(2)}) collective-permute-start(f32[16,2048]{1,0:T(8,128)S(1)} %get-tuple-element.9), channel_id=1, source_target_pairs={{8,0},{16,8},{24,16},{32,24},{40,32},{48,40},{56,48},{64,56},{72,6... | collective-permute-start | bytes 393224 | tf_op jit(solution)/shard_map/ppermute | solution.py:22
  48.4 0.0 copy-done.1
  48.5 0.9 fusion.21
  49.3 1.9 collective-permute-start.2
  51.3 1.3 collective-permute-start.3
  52.6 66.3 %all-reduce.3.cloned.1.call-done = f32[20,32768]{1,0:T(8,128)} async-done(((f32[20,32768]{1,0:T(8,128)}), f32[20,32768]{1,0:T(8,128)}) %all-reduce.3.cloned.1.call-update) | async-done | bytes 2621456 | tf_op jit(solution)/shard_map/psum | solution.py:44
  118.9 0.0 copy-done.3
  118.9 0.0 copy-start
  118.9 2.4 multiply_reduce_fusion.1
  121.3 0.0 copy-done.6
  121.3 71.1 %psum.30 = f32[20]{0:T(128)S(1)} all-reduce(f32[20]{0:T(128)S(1)} %multiply_reduce_fusion.1), channel_id=1, replica_groups=mesh['pix'=32,'shell'=8] {'pix'}, use_global_device_ids=true, to_apply=%region_5.0 | all-reduce | flops 20 | bytes 160 | tf_op jit(solution)/shard_map/psum | solution.py:45
  192.5 0.0 copy-done.5
  192.5 0.0 copy-done
  192.5 3.6 %subtract_reduce_fusion = (f32[]{:T(128)}, f32[20]{0:T(128)S(1)}) fusion(f32[20,32768]{1,0:T(8,128)S(1)} %copy-done, s32[20,32768]{1,0:T(8,128)} %param.12, f32[20]{0:T(128)S(1)} %broadcast_multiply_fusion, f32[20]{0:T(128)S(1)} %copy-done.5, f32[32768]{0:T(1024)S(1)} %copy-done.3), kind=kLoop, calls=%fused_computation.8 | loop fusion | flops 5242859 | bytes 5374196 | tf_op jit(solution)/shard_map/reduce_sum | solution.py:50
  196.1 74.9 %all-reduce = (f32[20]{0:T(128)S(1)}, f32[]{:T(128)}) all-reduce(f32[20]{0:T(128)S(1)} %get-tuple-element.3, f32[]{:T(128)} %get-tuple-element.2), channel_id=1, replica_groups=mesh['pix'=32,'shell'=8] {'pix'}, use_global_device_ids=true, to_apply=%region_3.0 | all-reduce | flops 21 | bytes 168 | tf_op jit(solution)/shard_map/psum | solution.py:45
  271.1 4.1 %multiply_subtract_fusion = f32[20,32768]{1,0:T(8,128)} fusion(f32[20,32768]{1,0:T(8,128)S(1)} %copy-done, s32[20,32768]{1,0:T(8,128)} %param.12, f32[20]{0:T(128)S(1)} %div.29, f32[32768]{0:T(1024)S(1)} %copy-done.3), kind=kLoop, calls=%fused_computation.9 | loop fusion | flops 2621440 | bytes 7995472 | tf_op jit(solution)/shard_map/sub | solution.py:52
  275.8 0.0 collective-permute-done
  275.8 0.0 collective-permute-done.1
  275.8 0.0 collective-permute-done.2
  275.8 0.0 collective-permute-done.3
  275.9 14.8 %fusion.11 = f32[16,32768]{1,0:T(8,128)} fusion(f32[16,32768]{1,0:T(8,128)} %copy-done.1, f32[16,2048]{1,0:T(8,128)} %collective-permute-done.1, f32[16,2048]{1,0:T(8,128)} %collective-permute-done, f32[1,32768]{1,0:T(1,128)} %collective-permute-done.3, f32[1,32768]{1,0:T(1,128)} %collective-permute-done.2, f32[4,20,16]{1,2,0:T(8,128)} %param.10, ...), kind=kOutput, calls=%fused_computation.22 | convolution fusion | flops 516947968 | bytes 7869504 | tf_op jit(solution)/shard_map/dot_general | solution.py:63
  (4 shorter events, 0.0 us)
Async XLA Ops:
  7.2 111.7 %all-reduce.3.cloned.1.call-start = ((), (), s32[]{:S(2)}) async-start(), calls=%async_computation | async-start | bytes 6291456 | tf_op jit(solution)/shard_map/psum | solution.py:44
  10.5 37.9 %copy-start.1 = (f32[16,32768]{1,0:T(8,128)}, f32[16,32768]{1,0:T(8,128)S(1)}, u32[]{:S(2)}) copy-start(f32[16,32768]{1,0:T(8,128)S(1)} %multiply_add_fusion) | copy-start | bytes 6291460
  21.4 11.4 %copy-start.4 = (s32[32768]{0:T(1024)S(1)}, s32[32768]{0:T(1024)}, u32[]{:S(2)}) copy-start(s32[32768]{0:T(1024)} %param.11) | copy-start | bytes 393220
  32.9 0.8 copy-start.2
  41.7 77.2 %copy-start.3 = (f32[32768]{0:T(1024)S(1)}, f32[32768]{0:T(1024)}, u32[]{:S(2)}) copy-start(f32[32768]{0:T(1024)} %param.13) | copy-start | bytes 393220
  41.8 79.6 %copy-start.6 = (f32[16]{0:T(128)S(1)}, f32[16]{0:T(128)}, u32[]{:S(2)}) copy-start(f32[16]{0:T(128)} %param.15) | copy-start | bytes 196
  41.8 150.7 %copy-start.5 = (f32[20]{0:T(128)S(1)}, f32[20]{0:T(128)}, u32[]{:S(2)}) copy-start(f32[20]{0:T(128)} %param.14) | copy-start | bytes 244
  41.8 234.0 %collective-permute-start = (f32[16,2048]{1,0:T(8,128)S(1)}, f32[16,2048]{1,0:T(8,128)}, u32[]{:S(2)}, u32[]{:S(2)}) collective-permute-start(f32[16,2048]{1,0:T(8,128)S(1)} %get-tuple-element.8), channel_id=1, source_target_pairs={{0,8},{8,16},{16,24},{24,32},{32,40},{40,48},{48,56},{56,64},{64,7... | collective-permute-start | bytes 393224 | tf_op jit(solution)/shard_map/ppermute | solution.py:20
  45.4 230.4 %collective-permute-start.1 = (f32[16,2048]{1,0:T(8,128)S(1)}, f32[16,2048]{1,0:T(8,128)}, u32[]{:S(2)}, u32[]{:S(2)}) collective-permute-start(f32[16,2048]{1,0:T(8,128)S(1)} %get-tuple-element.9), channel_id=1, source_target_pairs={{8,0},{16,8},{24,16},{32,24},{40,32},{48,40},{56,48},{64,56},{72,6... | collective-permute-start | bytes 393224 | tf_op jit(solution)/shard_map/ppermute | solution.py:22
  49.3 226.5 %collective-permute-start.2 = (f32[1,32768]{1,0:T(1,128)}, f32[1,32768]{1,0:T(1,128)}, u32[]{:S(2)}, u32[]{:S(2)}) collective-permute-start(f32[1,32768]{1,0:T(1,128)} %get-tuple-element.6), channel_id=1, source_target_pairs={{0,1},{1,2},{2,3},{3,4},{4,5},{5,6},{6,7},{8,9},{9,10},{10,11},{11... | collective-permute-start | bytes 393224 | tf_op jit(solution)/shard_map/ppermute | solution.py:20
  51.3 224.6 %collective-permute-start.3 = (f32[1,32768]{1,0:T(1,128)}, f32[1,32768]{1,0:T(1,128)}, u32[]{:S(2)}, u32[]{:S(2)}) collective-permute-start(f32[1,32768]{1,0:T(1,128)} %get-tuple-element.7), channel_id=1, source_target_pairs={{1,0},{2,1},{3,2},{4,3},{5,4},{6,5},{7,6},{9,8},{10,9},{11,10},{12... | collective-permute-start | bytes 393224 | tf_op jit(solution)/shard_map/ppermute | solution.py:22
  118.9 73.6 %copy-start = (f32[20,32768]{1,0:T(8,128)S(1)}, f32[20,32768]{1,0:T(8,128)}, u32[]{:S(2)}) copy-start(f32[20,32768]{1,0:T(8,128)} %all-reduce.3.cloned.1.call-done) | copy-start | bytes 7864324
Sparse Core Ops, SparseCore 0:
  41.9 76.9 all-reduce.2
where the time goes:
time: 299 us
  blocking collectives  146 us (49%)
  waiting for transfers between devices  66.4 us (22%)
  matrix products  25.7 us (9%)
  other arithmetic  20.8 us (7%)
  between operations  15.9 us (5%)
  local copies, waits for them, and re-layouts  14 us (5%)
  starting transfers between devices  9.87 us (3%)
    psum x2, blocking collectives, shards(): lax.psum((jnp.sum(mask[None, :] * proj, axis=1), jnp.sum(counted, axis=1)...  146 us
    psum x1, waiting for transfers between devices, shards(): proj = lax.psum(partial_proj, 'shell')  66.3 us
    dot_general x1, matrix products, shards(): lax.dot_general(flat, spread, (((0,), (0,)), ((), ())), precision=lax.Pre...  14.8 us
    reshape x1, local copies, waits for them, and re-layouts, shards(): every.reshape(classes, bins, pixels) * onehot[:, None, :]  11.4 us
    dot_general x1, matrix products, shards(): jnp.dot(flat, density, precision=lax.Precision.HIGHEST, preferred_element...  10.9 us
    reduce_sum x1, other arithmetic, shards(): jnp.sum(every.reshape(classes, bins, pixels) * onehot[:, None, :], axis=0)  8.02 us
  transfers between devices with their start and end apart: 5, of which 1 were waited for; matrix products, arithmetic and copies ran while one was open for 4% of the time, Pallas kernels for 0%

commit v1 on v0

--- a/solution.py
+++ b/solution.py
@@ -41,7 +41,8 @@
     )
     partial_proj = jnp.sum(every.reshape(classes, bins, pixels) * onehot[:, None, :], axis=0)
     counted = counts.astype(jnp.float32)
-    proj = lax.psum(partial_proj, "shell")
+    drive_the_slot = lambda mat, row_axis: jnp.sum(jax.lax.all_gather(mat, row_axis), axis=0)
+    proj = drive_the_slot(partial_proj, "shell")
     weighted, total = lax.psum(
         (jnp.sum(mask[None, :] * proj, axis=1), jnp.sum(counted, axis=1)), "pix"
     )

time: 299 us -> 355 us (1.19)
  waiting for transfers between devices: 66.4 us -> 115 us
  other arithmetic: 20.8 us -> 28.3 us
    all_gather x0 -> x1, waiting for transfers between devices: none -> 115 us  [shards(): jax.lax.all_gather(mat, row_axis)]
    psum x1 -> x0, waiting for transfers between devices: 66.3 us -> none  [shards(): proj = lax.psum(partial_proj, 'shell')]
    reduce_sum x0 -> x1, other arithmetic: none -> 9.46 us  [shards(): jnp.sum(jax.lax.all_gather(mat, row_axis), axis=0)]
  transfers between devices with their start and end apart: 5 -> 5, of which waited for: 1 -> 1; matrix products, arithmetic and copies ran while one was open for 4% -> 5% of each run, Pallas kernels for 0% -> 0%
where the time goes in v1:
time: 355 us; the launch traced here: 354 us
  blocking collectives  146 us (41%)
  waiting for transfers between devices  115 us (32%)
  other arithmetic  28.3 us (8%)
  matrix products  25.8 us (7%)
  between operations  15.9 us (4%)
  local copies, waits for them, and re-layouts  13.4 us (4%)
  starting transfers between devices  9.87 us (3%)
    psum x2, blocking collectives, shards(): lax.psum((jnp.sum(mask[None, :] * proj, axis=1), jnp.sum(counted, axis=1)...  146 us
    all_gather x1, waiting for transfers between devices, shards(): jax.lax.all_gather(mat, row_axis)  115 us
    dot_general x1, matrix products, shards(): lax.dot_general(flat, spread, (((0,), (0,)), ((), ())), precision=lax.Pre...  15 us
    reshape x1, local copies, waits for them, and re-layouts, shards(): every.reshape(classes, bins, pixels) * onehot[:, None, :]  11.4 us
    dot_general x1, matrix products, shards(): jnp.dot(flat, density, precision=lax.Precision.HIGHEST, preferred_element...  10.9 us
    reduce_sum x1, other arithmetic, shards(): jnp.sum(jax.lax.all_gather(mat, row_axis), axis=0)  9.46 us
    reduce_sum x1, other arithmetic, shards(): jnp.sum(every.reshape(classes, bins, pixels) * onehot[:, None, :], axis=0)  8.11 us
  transfers between devices with their start and end apart: 5, of which 1 were waited for; matrix products, arithmetic and copies ran while one was open for 5% of the time, Pallas kernels for 0%

profile of v1, /device:TPU:8, one launch (start us, length us, event | category | flops | bytes accessed | tf_op | source)
XLA Modules:
  0.0 354.4 jit_solution(8711617326727077758)
XLA Ops:
  7.2 0.0 all-gather.4.cloned.1.call-start
  7.2 0.8 copy.11
  8.0 0.1 reshape.36
  8.1 2.5 multiply_add_fusion
  10.5 0.0 copy-start
  10.5 10.9 %convolution_bitcast_fusion = f32[80,32768]{1,0:T(8,128)} fusion(f32[80,16]{0,1:T(8,128)S(1)} %reshape.36, f32[16,32768]{1,0:T(8,128)S(1)} %multiply_add_fusion), kind=kOutput, calls=%fused_computation | convolution fusion | flops 503316480 | bytes 12588032 | tf_op jit(solution)/shard_map/dot_general | solution.py:39
  21.4 0.0 copy-start.3
  21.4 11.4 %reshape.37 = f32[4,20,32768]{2,1,0:T(8,128)} reshape(f32[80,32768]{1,0:T(8,128)} %convolution_bitcast_fusion) | data formatting | bytes 20971520 | tf_op jit(solution)/shard_map/reshape | solution.py:42
  32.8 0.0 copy-done.3
  32.8 0.1 fusion.20
  32.9 0.0 copy-start.1
  32.9 8.1 %multiply_reduce_fusion = f32[20,32768]{1,0:T(8,128)} fusion(f32[4,20,32768]{2,1,0:T(8,128)} %reshape.37, f32[4,32768]{1,0:T(4,128)S(1)} %fusion.20), kind=kLoop, calls=%fused_computation.5 | loop fusion | flops 4587520 | bytes 13631488 | tf_op jit(solution)/shard_map/reduce_sum | solution.py:42
  41.0 0.0 copy-done.1
  41.0 0.0 all-gather.4.cloned.1.call-update
  41.1 3.5 collective-permute-start
  44.6 3.0 collective-permute-start.1
  47.6 0.0 copy-done
  47.6 0.9 fusion.21
  48.5 1.9 collective-permute-start.2
  50.4 0.0 copy-start.2
  50.4 1.4 collective-permute-start.3
  51.8 115.0 %all-gather.4.cloned.1.call-done = f32[8,20,32768]{2,1,0:T(8,128)} async-done(((f32[1,20,32768]{2,1,0:T(8,128)}), f32[8,20,32768]{2,1,0:T(8,128)}) %all-gather.4.cloned.1.call-update) | async-done | bytes 20971536 | tf_op jit(solution)/shard_map/all_gather | solution.py:44
  166.8 9.5 %reduce_sum.46 = f32[20,32768]{1,0:T(8,128)S(1)} reduce(f32[8,20,32768]{2,1,0:T(8,128)} %all-gather.4.cloned.1.call-done, f32[]{:T(128)} %constant.4.clone.1), dimensions={0}, to_apply=%region_1.0 | reduce | flops 4587520 | bytes 23592964 | tf_op jit(solution)/shard_map/reduce_sum | solution.py:44
  176.3 0.0 copy-done.2
  176.3 0.0 copy-start.5
  176.3 0.0 copy-start.4
  176.3 0.4 multiply_reduce_fusion.1
  176.8 0.2 copy-done.5
  177.0 71.1 %psum.22 = f32[20]{0:T(128)S(1)} all-reduce(f32[20]{0:T(128)S(1)} %multiply_reduce_fusion.1), channel_id=1, replica_groups=mesh['pix'=32,'shell'=8] {'pix'}, use_global_device_ids=true, to_apply=%region_5.0 | all-reduce | flops 20 | bytes 160 | tf_op jit(solution)/shard_map/psum | solution.py:46
  248.1 0.0 copy-done.4
  248.1 3.6 %subtract_reduce_fusion = (f32[]{:T(128)}, f32[20]{0:T(128)S(1)}) fusion(f32[20,32768]{1,0:T(8,128)S(1)} %reduce_sum.46, s32[20,32768]{1,0:T(8,128)} %param.12, f32[20]{0:T(128)S(1)} %broadcast_multiply_fusion, f32[20]{0:T(128)S(1)} %copy-done.4, f32[32768]{0:T(1024)S(1)} %copy-done.2), kind=kLoop, calls=%fused_computation.8 | loop fusion | flops 5242859 | bytes 5374196 | tf_op jit(solution)/shard_map/reduce_sum | solution.py:51
  251.8 74.9 %all-reduce = (f32[20]{0:T(128)S(1)}, f32[]{:T(128)}) all-reduce(f32[20]{0:T(128)S(1)} %get-tuple-element.3, f32[]{:T(128)} %get-tuple-element.2), channel_id=1, replica_groups=mesh['pix'=32,'shell'=8] {'pix'}, use_global_device_ids=true, to_apply=%region_3.0 | all-reduce | flops 21 | bytes 168 | tf_op jit(solution)/shard_map/psum | solution.py:46
  326.7 4.1 %multiply_subtract_fusion = f32[20,32768]{1,0:T(8,128)} fusion(f32[20,32768]{1,0:T(8,128)S(1)} %reduce_sum.46, s32[20,32768]{1,0:T(8,128)} %param.12, f32[20]{0:T(128)S(1)} %div.29, f32[32768]{0:T(1024)S(1)} %copy-done.2), kind=kLoop, calls=%fused_computation.9 | loop fusion | flops 2621440 | bytes 7995472 | tf_op jit(solution)/shard_map/sub | solution.py:53
  331.5 0.0 collective-permute-done
  331.5 0.0 collective-permute-done.1
  331.5 0.0 collective-permute-done.2
  331.5 0.0 collective-permute-done.3
  331.5 15.0 %fusion.11 = f32[16,32768]{1,0:T(8,128)} fusion(f32[16,32768]{1,0:T(8,128)} %copy-done, f32[16,2048]{1,0:T(8,128)} %collective-permute-done.1, f32[16,2048]{1,0:T(8,128)} %collective-permute-done, f32[1,32768]{1,0:T(1,128)} %collective-permute-done.3, f32[1,32768]{1,0:T(1,128)} %collective-permute-done.2, f32[4,20,16]{1,2,0:T(8,128)} %param.10, ...), kind=kOutput, calls=%fused_computation.22 | convolution fusion | flops 516947968 | bytes 7869504 | tf_op jit(solution)/shard_map/dot_general | solution.py:64
  (4 shorter events, 0.0 us)
Async XLA Ops:
  7.2 159.7 %all-gather.4.cloned.1.call-start = ((), (), s32[]{:S(2)}) async-start(), calls=%async_computation | async-start | bytes 28311552 | tf_op jit(solution)/shard_map/all_gather | solution.py:44
  10.5 37.1 %copy-start = (f32[16,32768]{1,0:T(8,128)}, f32[16,32768]{1,0:T(8,128)S(1)}, u32[]{:S(2)}) copy-start(f32[16,32768]{1,0:T(8,128)S(1)} %multiply_add_fusion) | copy-start | bytes 6291460
  21.4 11.4 %copy-start.3 = (s32[32768]{0:T(1024)S(1)}, s32[32768]{0:T(1024)}, u32[]{:S(2)}) copy-start(s32[32768]{0:T(1024)} %param.11) | copy-start | bytes 393220
  32.9 8.1 %copy-start.1 = (f32[4,32768]{1,0:T(4,128)}, f32[4,32768]{1,0:T(4,128)S(1)}, u32[]{:S(2)}) copy-start(f32[4,32768]{1,0:T(4,128)S(1)} %fusion.20) | copy-start | bytes 1572868
  41.1 290.4 %collective-permute-start = (f32[16,2048]{1,0:T(8,128)S(1)}, f32[16,2048]{1,0:T(8,128)}, u32[]{:S(2)}, u32[]{:S(2)}) collective-permute-start(f32[16,2048]{1,0:T(8,128)S(1)} %get-tuple-element.8), channel_id=1, source_target_pairs={{0,8},{8,16},{16,24},{24,32},{32,40},{40,48},{48,56},{56,64},{64,7... | collective-permute-start | bytes 393224 | tf_op jit(solution)/shard_map/ppermute | solution.py:20
  44.6 286.9 %collective-permute-start.1 = (f32[16,2048]{1,0:T(8,128)S(1)}, f32[16,2048]{1,0:T(8,128)}, u32[]{:S(2)}, u32[]{:S(2)}) collective-permute-start(f32[16,2048]{1,0:T(8,128)S(1)} %get-tuple-element.9), channel_id=1, source_target_pairs={{8,0},{16,8},{24,16},{32,24},{40,32},{48,40},{56,48},{64,56},{72,6... | collective-permute-start | bytes 393224 | tf_op jit(solution)/shard_map/ppermute | solution.py:22
  48.5 283.0 %collective-permute-start.2 = (f32[1,32768]{1,0:T(1,128)}, f32[1,32768]{1,0:T(1,128)}, u32[]{:S(2)}, u32[]{:S(2)}) collective-permute-start(f32[1,32768]{1,0:T(1,128)} %get-tuple-element.6), channel_id=1, source_target_pairs={{0,1},{1,2},{2,3},{3,4},{4,5},{5,6},{6,7},{8,9},{9,10},{10,11},{11... | collective-permute-start | bytes 393224 | tf_op jit(solution)/shard_map/ppermute | solution.py:20
  50.4 125.9 %copy-start.2 = (f32[32768]{0:T(1024)S(1)}, f32[32768]{0:T(1024)}, u32[]{:S(2)}) copy-start(f32[32768]{0:T(1024)} %param.13) | copy-start | bytes 393220
  50.4 281.1 %collective-permute-start.3 = (f32[1,32768]{1,0:T(1,128)}, f32[1,32768]{1,0:T(1,128)}, u32[]{:S(2)}, u32[]{:S(2)}) collective-permute-start(f32[1,32768]{1,0:T(1,128)} %get-tuple-element.7), channel_id=1, source_target_pairs={{1,0},{2,1},{3,2},{4,3},{5,4},{6,5},{7,6},{9,8},{10,9},{11,10},{12... | collective-permute-start | bytes 393224 | tf_op jit(solution)/shard_map/ppermute | solution.py:22
  176.3 0.7 copy-start.5
  176.3 71.8 %copy-start.4 = (f32[20]{0:T(128)S(1)}, f32[20]{0:T(128)}, u32[]{:S(2)}) copy-start(f32[20]{0:T(128)} %param.14) | copy-start | bytes 244
Sparse Core Ops, SparseCore 0:
  41.2 125.6 all-gather.3
